TPU v7x, 32 devices: a whole 2x2x4 slice. The times are simulated.
32 devices in a mesh: cells: 16 (over z, y, x), feat: 2 (over core).
Axes of the slice: x: 2, y: 2, z: 4, core: 2. Of those that a mesh axis runs over, the one named last changes fastest.
Arguments:
- features: float32 [32768, 4096], P('cells', 'feat'), may hold values from -6 to 6
- labels: int32 [32768], P('cells'), may hold values from 0 to 7
- weights: float32 [8, 4096], P(None, 'feat'), may hold values from -0.09375 to 0.09375
Outputs:
- new_weights: float32 [8, 4096], P(None, 'feat')
- new_logits: float32 [8, 32768], P(None, 'cells')
All inputs are finite; a program needn't handle non-finite values.
Results may differ from a plain program's by a relative error of at most 0.00018.
Values sent between devices are 32-bit elements; how exact they have to be, the bound alone decides.
A program may use at most 64 MiB of HBM per device.

v0:
```python
import jax
import jax.numpy as jnp
from jax import lax
from jax.sharding import PartitionSpec as P

ITERS = 2
HIGH = lax.Precision.HIGHEST
RIDGE = 0.01


def on_device(features, labels, weights):
    rows = features.shape[0]
    classes = weights.shape[0]
    count = rows * lax.axis_size("cells") * 1.0

    def row_sums(coeffs):
        local_rows = lax.dot_general(
            coeffs,
            features,
            (((1,), (1,)), ((), ())),
            precision=HIGH,
            preferred_element_type=jnp.float32,
        )
        summed = lax.psum(local_rows, "feat")
        return (summed, summed[classes:])

    def collect(terms):
        return lax.psum(jnp.dot(terms, features, precision=HIGH), "cells")

    def total(packed):
        return lax.psum(packed, "feat")

    def inner(left, right):
        return total(jnp.sum(left * right))

    logits, unused = row_sums(weights)
    expo = jnp.exp(logits)
    probs = expo / jnp.sum(expo, axis=0, keepdims=True)
    onehot = (labels[None, :] == jnp.arange(classes, dtype=jnp.int32)[:, None]).astype(jnp.float32)
    grad = collect(probs - onehot) / count + RIDGE * weights
    resid = -grad
    direction = resid
    rr_now = jnp.float32(0.0)
    rr_now = inner(resid, resid)
    step = jnp.zeros_like(weights)
    moved = jnp.zeros_like(logits)
    for it in range(ITERS):
        full_direction = direction
        image, unused = row_sums(full_direction)
        curv = probs * image - probs * jnp.sum(probs * image, axis=0, keepdims=True)
        product = collect(curv) / count + RIDGE * direction
        alpha = rr_now / inner(direction, product)
        step = step + alpha * direction
        moved = moved + alpha * image
        resid = resid - alpha * product
        if it + 1 < ITERS:
            rr_next = inner(resid, resid)
            direction = resid + rr_next / rr_now * direction
            rr_now = rr_next
    return (weights + step, logits + moved)


def solution(mesh):
    return jax.shard_map(
        on_device,
        mesh=mesh,
        in_specs=(P("cells", "feat"), P("cells"), P(None, "feat")),
        out_specs=(P(None, "feat"), P(None, "cells")),
        check_vma=False,
    )
```

profile of v0, /device:TPU:0, one launch (start us, length us, event | category | flops | bytes accessed | tf_op | source)
XLA Modules:
  0.0 500.8 jit_solution(12203118077418781199)
XLA Ops:
  7.2 0.0 all-reduce.8.cloned.1.call-start
  7.2 19.7 %fusion.21 = f32[8,2048]{1,0:T(8,128)} fusion(f32[8,2048]{1,0:T(8,128)} %param.5, f32[2048,2048]{1,0:T(8,128)} %param.3), kind=kOutput, calls=%fused_computation.32 | convolution fusion | flops 402653184 | bytes 16908288 | tf_op jit(solution)/shard_map/dot_general | solution.py:17
  26.9 0.0 all-reduce.8.cloned.1.call-update
  27.0 0.0 all-reduce.10.cloned.1.call-start
  27.0 20.5 %all-reduce.8.cloned.1.call-done = f32[8,2048]{1,0:T(8,128)} async-done(((f32[8,2048]{1,0:T(8,128)}), f32[8,2048]{1,0:T(8,128)}) %all-reduce.8.cloned.1.call-update) | async-done | bytes 65552 | tf_op jit(solution)/shard_map/psum | solution.py:24
  47.6 0.9 exponential_reduce_fusion
  48.5 14.2 %fusion.6 = f32[8,2048]{1,0:T(8,128)} fusion(f32[2048,2048]{1,0:T(8,128)} %param.3, s32[2048]{0:T(1024)S(1)} %copy-done.5, f32[8,2048]{1,0:T(8,128)} %all-reduce.8.cloned.1.call-done, f32[2048]{0:T(1024)S(1)} %exponential_reduce_fusion), kind=kOutput, calls=%fused_computation.16 | convolution fusion | flops 402718720 | bytes 16924672 | tf_op jit(solution)/shard_map/dot_general | solution.py:28
  62.6 0.0 all-reduce.10.cloned.1.call-update
  62.6 0.2 all-reduce.12.cloned.1.call-start
  62.9 104.6 %all-reduce.10.cloned.1.call-done = f32[8,2048]{1,0:T(8,128)} async-done(((f32[8,2048]{1,0:T(8,128)}), f32[8,2048]{1,0:T(8,128)}) %all-reduce.10.cloned.1.call-update) | async-done | bytes 65552 | tf_op jit(solution)/shard_map/psum | solution.py:28
  167.5 0.9 multiply_add_fusion.2
  168.3 17.7 %fusion.9 = f32[8,2048]{1,0:T(8,128)} fusion(f32[2048,2048]{1,0:T(8,128)} %param.3, f32[8,2048]{1,0:T(8,128)S(1)} %multiply_add_fusion.2), kind=kOutput, calls=%fused_computation.22 | convolution fusion | flops 402669568 | bytes 16908288 | tf_op jit(solution)/shard_map/dot_general | solution.py:17
  186.0 0.0 all-reduce.14.cloned.1.call-start
  186.1 16.9 %all-reduce.12.cloned.1.call-done = f32[8,2048]{1,0:T(8,128)} async-done(((f32[8,2048]{1,0:T(8,128)}), f32[8,2048]{1,0:T(8,128)}) %all-reduce.12.cloned.1.call-update) | async-done | bytes 65552 | tf_op jit(solution)/shard_map/psum | solution.py:24
  202.9 0.9 fusion.18
  203.8 12.1 %fusion.3 = f32[8,2048]{1,0:T(8,128)} fusion(f32[2048,2048]{1,0:T(8,128)} %param.3, f32[2048]{0:T(1024)S(1)} %fusion.18, f32[8,2048]{1,0:T(8,128)S(1)} %copy-done, f32[2048]{0:T(1024)S(1)} %exponential_reduce_fusion, f32[8,2048]{1,0:T(8,128)} %all-reduce.12.cloned.1.call-done), kind=kOutput, calls=%fused_computation.11 | convolution fusion | flops 402718720 | bytes 16990208 | tf_op jit(solution)/shard_map/dot_general | solution.py:28
  215.9 0.0 all-reduce.14.cloned.1.call-update
  215.9 0.0 all-reduce.16.cloned.1.call-start
  216.0 104.8 %all-reduce.14.cloned.1.call-done = f32[8,2048]{1,0:T(8,128)} async-done(((f32[8,2048]{1,0:T(8,128)}), f32[8,2048]{1,0:T(8,128)}) %all-reduce.14.cloned.1.call-update) | async-done | bytes 65552 | tf_op jit(solution)/shard_map/psum | solution.py:28
  320.8 1.5 multiply_reduce_fusion.2
  322.2 3.1 all-reduce
  326.6 1.5 multiply_reduce_fusion.1
  328.1 3.4 psum.76
  332.8 19.8 %fusion.14 = f32[8,2048]{1,0:T(8,128)} fusion(f32[2048,2048]{1,0:T(8,128)} %param.3, f32[8,2048]{1,0:T(8,128)S(1)} %multiply_add_fusion.2, f32[8,2048]{1,0:T(8,128)} %all-reduce.14.cloned.1.call-done, f32[]{:T(128)S(6)} %div.31, f32[]{:T(128)S(6)} %div.30), kind=kOutput, calls=%fused_computation.27 | convolution fusion | flops 402784256 | bytes 16973832 | tf_op jit(solution)/shard_map/dot_general | solution.py:17
  352.6 0.0 all-reduce.18.cloned.1.call-start
  352.6 16.9 %all-reduce.16.cloned.1.call-done = f32[8,2048]{1,0:T(8,128)} async-done(((f32[8,2048]{1,0:T(8,128)}), f32[8,2048]{1,0:T(8,128)}) %all-reduce.16.cloned.1.call-update) | async-done | bytes 65552 | tf_op jit(solution)/shard_map/psum | solution.py:24
  369.5 0.9 fusion.20
  370.5 12.1 %fusion = f32[8,2048]{1,0:T(8,128)} fusion(f32[2048,2048]{1,0:T(8,128)} %param.3, f32[2048]{0:T(1024)S(1)} %fusion.20, f32[8,2048]{1,0:T(8,128)S(1)} %copy-done, f32[2048]{0:T(1024)S(1)} %exponential_reduce_fusion, f32[8,2048]{1,0:T(8,128)} %all-reduce.16.cloned.1.call-done), kind=kOutput, calls=%fused_computation.3 | convolution fusion | flops 402718720 | bytes 16990208 | tf_op jit(solution)/shard_map/dot_general | solution.py:28
  382.6 104.8 %all-reduce.18.cloned.1.call-done = f32[8,2048]{1,0:T(8,128)} async-done(((f32[8,2048]{1,0:T(8,128)}), f32[8,2048]{1,0:T(8,128)}) %all-reduce.18.cloned.1.call-update) | async-done | bytes 65552 | tf_op jit(solution)/shard_map/psum | solution.py:28
  487.4 1.5 multiply_reduce_fusion
  488.9 3.1 psum.79
  493.3 0.7 add_add_fusion
  (15 shorter events, 0.1 us)
Async XLA Ops:
  7.2 160.3 %copy-start.2 = (f32[8,2048]{1,0:T(8,128)S(1)}, f32[8,2048]{1,0:T(8,128)}, u32[]{:S(2)}) copy-start(f32[8,2048]{1,0:T(8,128)} %param.5) | copy-start | bytes 196612
  7.2 41.3 %copy-start.5 = (s32[2048]{0:T(1024)S(1)}, s32[2048]{0:T(1024)}, u32[]{:S(2)}) copy-start(s32[2048]{0:T(1024)} %param.4) | copy-start | bytes 24580
  7.2 40.4 %all-reduce.8.cloned.1.call-start = ((), (), s32[]{:S(2)}) async-start(), calls=%async_computation | async-start | bytes 131072 | tf_op jit(solution)/shard_map/psum | solution.py:24
  27.0 140.5 %all-reduce.10.cloned.1.call-start = ((), (), s32[]{:S(2)}) async-start(), calls=%async_computation.1 | async-start | bytes 131072 | tf_op jit(solution)/shard_map/psum | solution.py:28
  48.4 154.5 %copy-start = (f32[8,2048]{1,0:T(8,128)S(1)}, f32[8,2048]{1,0:T(8,128)}, u32[]{:S(2)}) copy-start(f32[8,2048]{1,0:T(8,128)} %all-reduce.8.cloned.1.call-done) | copy-start | bytes 196612
  62.6 140.3 %all-reduce.12.cloned.1.call-start = ((), (), s32[]{:S(2)}) async-start(), calls=%async_computation.2 | async-start | bytes 131072 | tf_op jit(solution)/shard_map/psum | solution.py:24
  186.0 134.7 %all-reduce.14.cloned.1.call-start = ((), (), s32[]{:S(2)}) async-start(), calls=%async_computation.3 | async-start | bytes 131072 | tf_op jit(solution)/shard_map/psum | solution.py:28
  215.9 153.6 %all-reduce.16.cloned.1.call-start = ((), (), s32[]{:S(2)}) async-start(), calls=%async_computation.4 | async-start | bytes 131072 | tf_op jit(solution)/shard_map/psum | solution.py:24
  332.8 154.6 %copy-start.1 = (f32[8,2048]{1,0:T(8,128)S(1)}, f32[8,2048]{1,0:T(8,128)}, u32[]{:S(2)}) copy-start(f32[8,2048]{1,0:T(8,128)} %all-reduce.14.cloned.1.call-done) | copy-start | bytes 196612
  332.8 160.5 %copy-start.3 = (f32[8,2048]{1,0:T(8,128)S(1)}, f32[8,2048]{1,0:T(8,128)}, u32[]{:S(2)}) copy-start(f32[8,2048]{1,0:T(8,128)} %all-reduce.12.cloned.1.call-done) | copy-start | bytes 196612
  352.6 134.8 %all-reduce.18.cloned.1.call-start = ((), (), s32[]{:S(2)}) async-start(), calls=%async_computation.5 | async-start | bytes 131072 | tf_op jit(solution)/shard_map/psum | solution.py:28
  369.5 123.8 %copy-start.4 = (f32[8,2048]{1,0:T(8,128)S(1)}, f32[8,2048]{1,0:T(8,128)}, u32[]{:S(2)}) copy-start(f32[8,2048]{1,0:T(8,128)} %all-reduce.16.cloned.1.call-done) | copy-start | bytes 196612
Sparse Core Ops, SparseCore 0:
  27.1 20.4 all-reduce.7
  62.8 104.6 all-reduce.9
  186.1 16.7 all-reduce.11
  216.0 104.6 all-reduce.13
  352.7 16.7 all-reduce.15
  382.7 104.6 all-reduce.17
where the time goes:
time: 501 us
  waiting for transfers between devices  369 us (74%)
  matrix products  95.5 us (19%)
  between operations  18.2 us (4%)
  blocking collectives  9.52 us (2%)
  other arithmetic  8.63 us (2%)
    psum x3, waiting for transfers between devices, collect(): return lax.psum(jnp.dot(terms, features, precision=HIGH), 'cells')  314 us
    dot_general x3, matrix products, row_sums(): lax.dot_general(coeffs, features, (((1,), (1,)), ((), ())), precision=HIG...  57.1 us
    psum x3, waiting for transfers between devices, row_sums(): summed = lax.psum(local_rows, 'feat')  54.3 us
    dot_general x3, matrix products, collect(): return lax.psum(jnp.dot(terms, features, precision=HIGH), 'cells')  38.3 us
  transfers between devices with their start and end apart: 6, of which 6 were waited for; matrix products, arithmetic and copies ran while one was open for 0% of the time, Pallas kernels for 0%

commit v1 on v0

--- a/solution.py
+++ b/solution.py
@@ -1,3 +1,4 @@
+import functools
 import jax
 import jax.numpy as jnp
 from jax import lax
@@ -6,6 +7,13 @@
 ITERS = 2
 HIGH = lax.Precision.HIGHEST
 RIDGE = 0.01
+
+
+def _feed_leaf(body, mesh_name):
+    return lax.all_gather(body, mesh_name).sum(axis=0)
+
+
+links_read = functools.partial(_feed_leaf, mesh_name="cells")
 
 
 def on_device(features, labels, weights):
@@ -25,7 +33,7 @@
         return (summed, summed[classes:])
 
     def collect(terms):
-        return lax.psum(jnp.dot(terms, features, precision=HIGH), "cells")
+        return links_read(jnp.dot(terms, features, precision=HIGH))
 
     def total(packed):
         return lax.psum(packed, "feat")

time: 501 us -> 354 us (0.71)
  waiting for transfers between devices: 369 us -> 223 us
    psum x3 -> x0, waiting for transfers between devices: 314 us -> none  [collect(): return lax.psum(jnp.dot(terms, features, precision=HIGH), 'cells')]
    all_gather x0 -> x3, waiting for transfers between devices: none -> 169 us  [_feed_leaf(): return lax.all_gather(body, mesh_name).sum(axis=0)]
where the time goes in v1:
time: 354 us
  waiting for transfers between devices  223 us (63%)
  matrix products  93.4 us (26%)
  between operations  18.2 us (5%)
  blocking collectives  9.52 us (3%)
  other arithmetic  9.12 us (3%)
    all_gather x3, waiting for transfers between devices, _feed_leaf(): return lax.all_gather(body, mesh_name).sum(axis=0)  169 us
    dot_general x3, matrix products, row_sums(): lax.dot_general(coeffs, features, (((1,), (1,)), ((), ())), precision=HIG...  55.1 us
    psum x3, waiting for transfers between devices, row_sums(): summed = lax.psum(local_rows, 'feat')  53.9 us
    dot_general x3, matrix products, collect(): return links_read(jnp.dot(terms, features, precision=HIGH))  38.3 us
    psum x3, blocking collectives, total(): return lax.psum(packed, 'feat')  9.52 us
  transfers between devices with their start and end apart: 6, of which 6 were waited for; matrix products, arithmetic and copies ran while one was open for 0% of the time, Pallas kernels for 0%

profile of v1, /device:TPU:0, one launch (start us, length us, event | category | flops | bytes accessed | tf_op | source)
XLA Modules:
  0.0 353.7 jit_solution(5152977687732616689)
XLA Ops:
  7.2 0.0 all-reduce.5.cloned.1.call-start
  7.2 19.7 %fusion.21 = f32[8,2048]{1,0:T(8,128)} fusion(f32[8,2048]{1,0:T(8,128)} %param.5, f32[2048,2048]{1,0:T(8,128)} %param.3), kind=kOutput, calls=%fused_computation.35 | convolution fusion | flops 402653184 | bytes 16908288 | tf_op jit(solution)/shard_map/dot_general | solution.py:25
  26.9 0.0 all-reduce.5.cloned.1.call-update
  27.0 0.0 all-gather.7.cloned.1.call-start
  27.0 20.5 %all-reduce.5.cloned.1.call-done = f32[8,2048]{1,0:T(8,128)} async-done(((f32[8,2048]{1,0:T(8,128)}), f32[8,2048]{1,0:T(8,128)}) %all-reduce.5.cloned.1.call-update) | async-done | bytes 65552 | tf_op jit(solution)/shard_map/psum | solution.py:32
  47.6 0.9 exponential_reduce_fusion
  48.5 14.2 %fusion.6 = f32[8,2048]{1,0:T(8,128)} fusion(f32[2048,2048]{1,0:T(8,128)} %param.3, s32[2048]{0:T(1024)S(1)} %copy-done.4, f32[8,2048]{1,0:T(8,128)} %all-reduce.5.cloned.1.call-done, f32[2048]{0:T(1024)S(1)} %exponential_reduce_fusion), kind=kOutput, calls=%fused_computation.19 | convolution fusion | flops 402718720 | bytes 16924672 | tf_op jit(solution)/shard_map/dot_general | solution.py:36
  62.6 0.2 all-reduce.7.cloned.1.call-start
  62.9 56.2 %all-gather.7.cloned.1.call-done = f32[128,2048]{1,0:T(8,128)} async-done(((f32[8,2048]{1,0:T(8,128)}), f32[128,2048]{1,0:T(8,128)}) %all-gather.7.cloned.1.call-update) | async-done | bytes 1048592 | tf_op jit(solution)/shard_map/all_gather | solution.py:13
  119.1 1.3 bitcast_reduce_fusion.2
  120.4 17.7 %fusion.9 = f32[8,2048]{1,0:T(8,128)} fusion(f32[2048,2048]{1,0:T(8,128)} %param.3, f32[8,2048]{1,0:T(8,128)S(1)} %multiply_add_fusion.2), kind=kOutput, calls=%fused_computation.25 | convolution fusion | flops 402669568 | bytes 16908288 | tf_op jit(solution)/shard_map/dot_general | solution.py:25
  138.1 0.0 all-gather.9.cloned.1.call-start
  138.1 16.7 %all-reduce.7.cloned.1.call-done = f32[8,2048]{1,0:T(8,128)} async-done(((f32[8,2048]{1,0:T(8,128)}), f32[8,2048]{1,0:T(8,128)}) %all-reduce.7.cloned.1.call-update) | async-done | bytes 65552 | tf_op jit(solution)/shard_map/psum | solution.py:32
  154.8 0.9 fusion.18
  155.7 12.1 %fusion.3 = f32[8,2048]{1,0:T(8,128)} fusion(f32[2048,2048]{1,0:T(8,128)} %param.3, f32[2048]{0:T(1024)S(1)} %fusion.18, f32[8,2048]{1,0:T(8,128)S(1)} %copy-done, f32[2048]{0:T(1024)S(1)} %exponential_reduce_fusion, f32[8,2048]{1,0:T(8,128)} %all-reduce.7.cloned.1.call-done), kind=kOutput, calls=%fused_computation.14 | convolution fusion | flops 402718720 | bytes 16990208 | tf_op jit(solution)/shard_map/dot_general | solution.py:36
  167.8 0.0 all-reduce.9.cloned.1.call-start
  167.9 56.4 %all-gather.9.cloned.1.call-done = f32[128,2048]{1,0:T(8,128)} async-done(((f32[8,2048]{1,0:T(8,128)}), f32[128,2048]{1,0:T(8,128)}) %all-gather.9.cloned.1.call-update) | async-done | bytes 1048592 | tf_op jit(solution)/shard_map/all_gather | solution.py:13
  224.3 1.3 bitcast_reduce_fusion.1
  225.5 0.6 multiply_reduce_fusion.2
  226.2 3.1 all-reduce
  230.6 0.6 multiply_reduce_fusion.1
  231.2 3.4 psum.53
  235.9 17.7 %fusion.14 = f32[8,2048]{1,0:T(8,128)} fusion(f32[2048,2048]{1,0:T(8,128)} %param.3, f32[8,2048]{1,0:T(8,128)S(1)} %multiply_add_fusion.2, f32[8,2048]{1,0:T(8,128)S(1)} %bitcast_reduce_fusion.1, f32[]{:T(128)S(6)} %div.31, f32[]{:T(128)S(6)} %div.30), kind=kOutput, calls=%fused_computation.30 | convolution fusion | flops 402784256 | bytes 16973832 | tf_op jit(solution)/shard_map/dot_general | solution.py:25
  253.6 0.0 all-gather.11.cloned.1.call-start
  253.7 16.7 %all-reduce.9.cloned.1.call-done = f32[8,2048]{1,0:T(8,128)} async-done(((f32[8,2048]{1,0:T(8,128)}), f32[8,2048]{1,0:T(8,128)}) %all-reduce.9.cloned.1.call-update) | async-done | bytes 65552 | tf_op jit(solution)/shard_map/psum | solution.py:32
  270.3 0.9 fusion.20
  271.3 12.1 %fusion = f32[8,2048]{1,0:T(8,128)} fusion(f32[2048,2048]{1,0:T(8,128)} %param.3, f32[2048]{0:T(1024)S(1)} %fusion.20, f32[8,2048]{1,0:T(8,128)S(1)} %copy-done, f32[2048]{0:T(1024)S(1)} %exponential_reduce_fusion, f32[8,2048]{1,0:T(8,128)} %all-reduce.9.cloned.1.call-done), kind=kOutput, calls=%fused_computation.6 | convolution fusion | flops 402718720 | bytes 16990208 | tf_op jit(solution)/shard_map/dot_general | solution.py:36
  283.4 56.5 %all-gather.11.cloned.1.call-done = f32[128,2048]{1,0:T(8,128)} async-done(((f32[8,2048]{1,0:T(8,128)}), f32[128,2048]{1,0:T(8,128)}) %all-gather.11.cloned.1.call-update) | async-done | bytes 1048592 | tf_op jit(solution)/shard_map/all_gather | solution.py:13
  339.9 1.3 bitcast_reduce_fusion
  341.1 0.6 multiply_reduce_fusion
  341.8 3.1 psum.55
  346.2 0.7 add_add_fusion
  (16 shorter events, 0.1 us)
Async XLA Ops:
  7.2 113.2 %copy-start.1 = (f32[8,2048]{1,0:T(8,128)S(1)}, f32[8,2048]{1,0:T(8,128)}, u32[]{:S(2)}) copy-start(f32[8,2048]{1,0:T(8,128)} %param.5) | copy-start | bytes 196612
  7.2 41.3 %copy-start.4 = (s32[2048]{0:T(1024)S(1)}, s32[2048]{0:T(1024)}, u32[]{:S(2)}) copy-start(s32[2048]{0:T(1024)} %param.4) | copy-start | bytes 24580
  7.2 40.4 %all-reduce.5.cloned.1.call-start = ((), (), s32[]{:S(2)}) async-start(), calls=%async_computation | async-start | bytes 131072 | tf_op jit(solution)/shard_map/psum | solution.py:32
  27.0 92.1 %all-gather.7.cloned.1.call-start = ((), (), s32[]{:S(2)}) async-start(), calls=%async_computation.3 | async-start | bytes 1114112 | tf_op jit(solution)/shard_map/all_gather | solution.py:13
  48.4 106.4 %copy-start = (f32[8,2048]{1,0:T(8,128)S(1)}, f32[8,2048]{1,0:T(8,128)}, u32[]{:S(2)}) copy-start(f32[8,2048]{1,0:T(8,128)} %all-reduce.5.cloned.1.call-done) | copy-start | bytes 196612
  62.6 92.2 %all-reduce.7.cloned.1.call-start = ((), (), s32[]{:S(2)}) async-start(), calls=%async_computation.1 | async-start | bytes 131072 | tf_op jit(solution)/shard_map/psum | solution.py:32
  138.1 86.2 %all-gather.9.cloned.1.call-start = ((), (), s32[]{:S(2)}) async-start(), calls=%async_computation.4 | async-start | bytes 1114112 | tf_op jit(solution)/shard_map/all_gather | solution.py:13
  167.8 102.5 %all-reduce.9.cloned.1.call-start = ((), (), s32[]{:S(2)}) async-start(), calls=%async_computation.2 | async-start | bytes 131072 | tf_op jit(solution)/shard_map/psum | solution.py:32
  235.9 110.3 %copy-start.2 = (f32[8,2048]{1,0:T(8,128)S(1)}, f32[8,2048]{1,0:T(8,128)}, u32[]{:S(2)}) copy-start(f32[8,2048]{1,0:T(8,128)} %all-reduce.7.cloned.1.call-done) | copy-start | bytes 196612
  253.6 86.2 %all-gather.11.cloned.1.call-start = ((), (), s32[]{:S(2)}) async-start(), calls=%async_computation.5 | async-start | bytes 1114112 | tf_op jit(solution)/shard_map/all_gather | solution.py:13
  270.3 75.8 %copy-start.3 = (f32[8,2048]{1,0:T(8,128)S(1)}, f32[8,2048]{1,0:T(8,128)}, u32[]{:S(2)}) copy-start(f32[8,2048]{1,0:T(8,128)} %all-reduce.9.cloned.1.call-done) | copy-start | bytes 196612
Sparse Core Ops, SparseCore 0:
  27.1 20.4 all-reduce.4
  62.8 56.2 all-gather.6
  138.2 16.5 all-reduce.6
  167.9 56.2 all-gather.8
  253.8 16.5 all-reduce.8
  283.5 56.2 all-gather.10
